TPU v7x, 256 devices: a whole 4x4x8 slice. The times are simulated.
256 devices in a mesh: trow: 32 (over z, x), tcol: 8 (over y, core).
Axes of the slice: x: 4, y: 4, z: 8, core: 2. Of those that a mesh axis runs over, the one named last changes fastest.
Arguments:
- query: bfloat16 [64, 512, 1152], P('trow', 'tcol'), may hold values from -64 to 64
- key: bfloat16 [64, 512, 1152], P('trow', 'tcol'), may hold values from -6 to 6
- value: bfloat16 [64, 512, 1152], P('trow', 'tcol'), may hold values from -6 to 6
- control: bfloat16 [64, 512, 1152], P('trow', 'tcol'), may hold values from -6 to 6
- kernel: float32 [3, 3, 1152], replicated, may hold values from -3 to 3
- grad_out: bfloat16 [64, 512, 1152], P('trow', 'tcol'), may hold values from -96 to 96
- detail_blocks: int32 [32, 8, 8], P('trow'), may hold values from -1 to 0, as said below
Outputs:
- grad_query: bfloat16 [64, 512, 1152], P('trow', 'tcol')
- grad_key: bfloat16 [64, 512, 1152], P('trow', 'tcol')
- grad_value: bfloat16 [64, 512, 1152], P('trow', 'tcol')
- grad_control: bfloat16 [64, 512, 1152], P('trow', 'tcol')
- grad_kernel: float32 [3, 3, 1152], replicated
Inputs may be any that keep to these rules, and one draw needn't show every extreme that they name: `detail_blocks`: entry [i, j, p] is the key block of tile (i, p) that tile (i, j) also attends to, or -1 for none; entry [i, j, j] is -1; each tile names blocks of 1 to 7 other tiles, and in every tile row one tile names a block of each of the other 7 tiles.
All inputs are finite; a program needn't handle non-finite values.
Results may differ from a plain program's by a relative error of at most 0.0095.
Values may be sent and summed in bfloat16 or wider, within the bound.
A program may use at most 128 MiB of HBM per device.

v0:
```python
import math
import jax
import jax.numpy as jnp
from jax import lax
from jax.sharding import PartitionSpec as P

HEADS = 16
HEAD_DIM = 72
BLOCK = 128
NEG = -1e30


def with_halo(block, sides, width):
    for axis, dim in sides:
        count = lax.axis_size(axis)
        forward = [(i, i + 1) for i in range(count - 1)]
        backward = [(target, source) for source, target in forward]
        low = lax.ppermute(
            lax.slice_in_dim(block, block.shape[dim] - width, None, axis=dim), axis, forward
        )
        high = lax.ppermute(lax.slice_in_dim(block, 0, width, axis=dim), axis, backward)
        block = jnp.concatenate([low, block, high], axis=dim)
    return block


def from_behind(shard, axis, by):
    length = lax.axis_size(axis)
    pairs = [(i, i + by) for i in range(length) if 0 <= i + by < length]
    return lax.ppermute(shard, axis, pairs)


def conv_taps(padded, kernel, rows, cols):
    total = jnp.zeros((rows, cols, padded.shape[2]), jnp.float32)
    for row_off in range(3):
        for col_off in range(3):
            total = (
                total
                + kernel[row_off, col_off][None, None, :]
                * padded[row_off : row_off + rows, col_off : col_off + cols]
            )
    return total


def conv_back(padded, kernel, rows, cols):
    total = jnp.zeros((rows, cols, padded.shape[2]), jnp.float32)
    for row_off in range(3):
        for col_off in range(3):
            total = (
                total
                + kernel[row_off, col_off][None, None, :]
                * padded[2 - row_off : 2 - row_off + rows, 2 - col_off : 2 - col_off + cols]
            )
    return total


def attend_group(queries, grads, keys, values, key_live):
    inv_root = HEAD_DIM ** (-0.5)
    scores = (
        jnp.einsum("qhd,khd->hqk", queries, keys, preferred_element_type=jnp.float32) * inv_root
    )
    scores = jnp.where(key_live[None, None, :], scores, NEG)
    row_top = jnp.max(scores, axis=2, keepdims=True)
    raised = jnp.exp(scores - row_top)
    weights = raised / jnp.sum(raised, axis=2, keepdims=True)
    weights_bf = weights.astype(jnp.bfloat16)
    attn_out = jnp.einsum("hqk,khd->qhd", weights_bf, values, preferred_element_type=jnp.float32)
    row_delta = jnp.sum(grads.astype(jnp.float32) * attn_out, axis=2)
    grad_weights = jnp.einsum("qhd,khd->hqk", grads, values, preferred_element_type=jnp.float32)
    grad_scores = weights * (grad_weights - jnp.transpose(row_delta)[:, :, None])
    grad_scores_bf = grad_scores.astype(jnp.bfloat16)
    grad_q = (
        jnp.einsum("hqk,khd->qhd", grad_scores_bf, keys, preferred_element_type=jnp.float32)
        * inv_root
    )
    grad_k = (
        jnp.einsum("hqk,qhd->khd", grad_scores_bf, queries, preferred_element_type=jnp.float32)
        * inv_root
    )
    grad_v = jnp.einsum("hqk,qhd->khd", weights_bf, grads, preferred_element_type=jnp.float32)
    return (grad_q, grad_k, grad_v)


def per_device(query, key, value, control, kernel, grad_out, detail_blocks):
    tile_rows, tile_column_count, channels = query.shape
    tile_tokens = tile_rows * tile_column_count
    tile_blocks = tile_tokens // BLOCK
    row_count = lax.axis_size("trow")
    col_count = lax.axis_size("tcol")
    my_row = lax.axis_index("trow")
    my_col = lax.axis_index("tcol")
    control_ext = with_halo(control, (("trow", 0), ("tcol", 1)), 1).astype(jnp.float32)
    v_ctrl = (
        value.astype(jnp.float32) + conv_taps(control_ext, kernel, tile_rows, tile_column_count)
    ).astype(jnp.bfloat16)
    query_flat = query.reshape(tile_tokens, channels)
    key_flat = key.reshape(tile_tokens, channels)
    value_flat = v_ctrl.reshape(tile_tokens, channels)
    grad_flat = grad_out.reshape(tile_tokens, channels)
    above = from_behind((key_flat, value_flat), "trow", 1)
    below = from_behind((key_flat, value_flat), "trow", -1)
    pattern = detail_blocks[0]
    wanted = lax.dynamic_index_in_dim(pattern, my_col, 0, keepdims=False)
    asked = lax.dynamic_index_in_dim(pattern, my_col, 1, keepdims=False)
    slot_ids = jnp.arange(col_count - 1, dtype=jnp.int32)
    others = slot_ids + (slot_ids >= my_col).astype(jnp.int32)
    wanted_others = wanted[others]
    row_keys, row_values = (
        lax.all_gather(key_flat, "tcol", axis=0, tiled=True),
        lax.all_gather(value_flat, "tcol", axis=0, tiled=True),
    )
    picked = others * tile_blocks + jnp.maximum(wanted_others, 0)
    detail_keys = row_keys.reshape(col_count * tile_blocks, BLOCK, channels)[picked]
    detail_values = row_values.reshape(col_count * tile_blocks, BLOCK, channels)[picked]
    detail_count = (col_count - 1) * BLOCK
    all_keys = jnp.concatenate(
        [key_flat, above[0], below[0], detail_keys.reshape(detail_count, channels)], axis=0
    )
    all_values = jnp.concatenate(
        [value_flat, above[1], below[1], detail_values.reshape(detail_count, channels)], axis=0
    )
    key_live = jnp.concatenate(
        [
            jnp.ones((tile_tokens,), bool),
            jnp.full((tile_tokens,), my_row >= 1),
            jnp.full((tile_tokens,), my_row + 1 < row_count),
            jnp.repeat(wanted_others >= 0, BLOCK),
        ],
        axis=0,
    )
    head_group = math.gcd(HEADS, 4)
    col_span = head_group * HEAD_DIM
    query_parts = []
    key_parts = []
    value_parts = []
    for group_index in range(HEADS // head_group):
        low = group_index * col_span
        high = low + col_span
        grad_q, grad_k, grad_v = attend_group(
            query_flat[:, low:high].reshape(-1, head_group, HEAD_DIM),
            grad_flat[:, low:high].reshape(-1, head_group, HEAD_DIM),
            all_keys[:, low:high].reshape(-1, head_group, HEAD_DIM),
            all_values[:, low:high].reshape(-1, head_group, HEAD_DIM),
            key_live,
        )
        query_parts.append(grad_q.reshape(-1, col_span))
        key_parts.append(grad_k.reshape(-1, col_span))
        value_parts.append(grad_v.reshape(-1, col_span))
    query_gradient_total = jnp.concatenate(query_parts, axis=1)
    grad_k_all = jnp.concatenate(key_parts, axis=1)
    grad_v_all = jnp.concatenate(value_parts, axis=1)
    up_terms = from_behind(
        (grad_k_all[tile_tokens : 2 * tile_tokens], grad_v_all[tile_tokens : 2 * tile_tokens]),
        "trow",
        -1,
    )
    down_terms = from_behind(
        (
            grad_k_all[2 * tile_tokens : 3 * tile_tokens],
            grad_v_all[2 * tile_tokens : 3 * tile_tokens],
        ),
        "trow",
        1,
    )
    slot_k = (
        grad_k_all[3 * tile_tokens :].reshape(col_count - 1, BLOCK, channels).astype(jnp.bfloat16)
    )
    slot_v = (
        grad_v_all[3 * tile_tokens :].reshape(col_count - 1, BLOCK, channels).astype(jnp.bfloat16)
    )
    detail_k = jnp.zeros((col_count, BLOCK, channels), jnp.bfloat16).at[others].set(slot_k)
    detail_v = jnp.zeros((col_count, BLOCK, channels), jnp.bfloat16).at[others].set(slot_v)
    returned_keys, returned_values = (
        lax.all_to_all(detail_k, "tcol", split_axis=0, concat_axis=0, tiled=True),
        lax.all_to_all(detail_v, "tcol", split_axis=0, concat_axis=0, tiled=True),
    )
    tile_owner_lookup = (
        asked[None, :] == jnp.arange(tile_blocks, dtype=jnp.int32)[:, None]
    ).astype(jnp.bfloat16)
    served_keys = jnp.einsum(
        "ev,vsw->esw", tile_owner_lookup, returned_keys, preferred_element_type=jnp.float32
    ).reshape(tile_tokens, channels)
    served_values = jnp.einsum(
        "ev,vsw->esw", tile_owner_lookup, returned_values, preferred_element_type=jnp.float32
    ).reshape(tile_tokens, channels)
    grad_key = (grad_k_all[:tile_tokens] + up_terms[0] + down_terms[0] + served_keys).astype(
        jnp.bfloat16
    )
    grad_value = (grad_v_all[:tile_tokens] + up_terms[1] + down_terms[1] + served_values).astype(
        jnp.bfloat16
    )
    grad_value_img = grad_value.reshape(tile_rows, tile_column_count, channels)
    value_ext = with_halo(grad_value_img, (("trow", 0), ("tcol", 1)), 1).astype(jnp.float32)
    grad_control = conv_back(value_ext, kernel, tile_rows, tile_column_count).astype(jnp.bfloat16)
    grad_value_f = grad_value_img.astype(jnp.float32)
    kernel_rows = []
    for row_off in range(3):
        kernel_cols = []
        for col_off in range(3):
            kernel_cols.append(
                jnp.sum(
                    control_ext[
                        row_off : row_off + tile_rows, col_off : col_off + tile_column_count
                    ]
                    * grad_value_f,
                    axis=(0, 1),
                )
            )
        kernel_rows.append(jnp.stack(kernel_cols, axis=0))
    grad_kernel = lax.psum(jnp.stack(kernel_rows, axis=0), ("trow", "tcol"))
    grad_query = query_gradient_total.astype(jnp.bfloat16).reshape(
        tile_rows, tile_column_count, channels
    )
    return (
        grad_query,
        grad_key.reshape(tile_rows, tile_column_count, channels),
        grad_value_img,
        grad_control,
        grad_kernel,
    )


def solution(mesh):
    return jax.shard_map(
        per_device,
        mesh=mesh,
        in_specs=(
            P("trow", "tcol", None),
            P("trow", "tcol", None),
            P("trow", "tcol", None),
            P("trow", "tcol", None),
            P(),
            P("trow", "tcol", None),
            P("trow", None, None),
        ),
        out_specs=(
            P("trow", "tcol", None),
            P("trow", "tcol", None),
            P("trow", "tcol", None),
            P("trow", "tcol", None),
            P(),
        ),
        check_vma=False,
    )
```

profile of v0, /device:TPU:1, one launch (start us, length us, event | category | flops | bytes accessed | tf_op | source)
XLA Modules:
  0.0 365.8 jit_solution(7707213717412692028)
XLA Ops:
  9.3 5.3 %collective-permute-start = (bf16[128,1152]{1,0:T(8,128)(2,1)}, bf16[128,1152]{1,0:T(8,128)(2,1)}, u32[]{:S(2)}, u32[]{:S(2)}) collective-permute-start(bf16[128,1152]{1,0:T(8,128)(2,1)} %bitcast.267), channel_id=1, source_target_pairs={{0,8},{8,16},{16,24},{24,32},{32,40},{40,48},{48,56},{56,64},{64,7... | collective-permute-start | bytes 884744 | tf_op jit(solution)/shard_map/ppermute | solution.py:29
  15.6 2.6 collective-permute-start.2
  24.2 4.9 %collective-permute-start.5 = (bf16[4,1,1152]{2,1,0:T(2,128)(2,1)S(1)}, bf16[4,1,1152]{2,1,0:T(2,128)(2,1)S(1)}, u32[]{:S(2)}, u32[]{:S(2)}) collective-permute-start(bf16[4,1,1152]{2,1,0:T(2,128)(2,1)S(1)} %get-tuple-element.43), channel_id=1, source_target_pairs={{1,0},{2,1},{3,2},{4,3},{5,4},{6,5},{7,6},{9,8},{10,9},{11,10},{12... | collective-permute-start | bytes 27656 | tf_op jit(solution)/shard_map/ppermute | solution.py:21
  29.1 2.8 collective-permute-start.4
  40.7 5.8 %collective-permute-start.6 = (bf16[128,1152]{1,0:T(8,128)(2,1)}, bf16[128,1152]{1,0:T(8,128)(2,1)}, u32[]{:S(2)}, u32[]{:S(2)}) collective-permute-start(bf16[128,1152]{1,0:T(8,128)(2,1)} %bitcast.12), channel_id=1, source_target_pairs={{0,8},{8,16},{16,24},{24,32},{32,40},{40,48},{48,56},{56,64},{64,7... | collective-permute-start | bytes 884744 | tf_op jit(solution)/shard_map/ppermute | solution.py:29
  46.5 2.7 gather_fusion.1
  50.6 3.0 fusion.101
  55.9 4.0 %fusion.108 = (f32[4,128]{1,0:T(4,128)S(1)}, f32[4,128,1280]{1,2,0:T(8,128)}) fusion(bf16[1280,4,72]{0,2,1:T(8,128)(2,1)} %bitcast.257, bf16[128,4,72]{0,2,1:T(8,128)(2,1)S(1)} %bitcast.287, pred[1280]{0:T(1024)(128)(4,1)S(1)} %copy-done.47), kind=kOutput, calls=%fused_computation.197 | convolution fusion | flops 96994560 | bytes 3435776 | tf_op jit(solution)/shard_map/sub | solution.py:63
  59.9 2.7 fusion.109
  70.3 3.0 copy.87
  78.5 2.7 copy.88
  81.3 3.6 fusion.107
  90.0 2.8 copy.89
  92.9 3.5 fusion.106
  101.5 2.8 copy.90
  104.3 8.9 %concatenate.51 = f32[1280,1152]{1,0:T(8,128)} concatenate(f32[1280,288]{1,0:T(8,128)} %copy.87, f32[1280,288]{1,0:T(8,128)} %copy.88, f32[1280,288]{1,0:T(8,128)} %copy.89, f32[1280,288]{1,0:T(8,128)} %copy.90), dimensions={1} | concatenate | bytes 11796480 | tf_op jit(solution)/shard_map/concatenate | solution.py:150
  113.1 3.7 %slice.404 = bf16[896,1152]{1,0:T(8,128)(2,1)} slice(f32[1280,1152]{1,0:T(8,128)} %concatenate.51), slice={[384:1280], [0:1152]} | slice | bytes 4128768 | tf_op jit(solution)/shard_map/slice | solution.py:168
  116.8 2.4 fusion.98
  119.2 3.7 %collective-permute-start.11 = (f32[128,1152]{1,0:T(8,128)}, f32[128,1152]{1,0:T(8,128)}, u32[]{:S(2)}, u32[]{:S(2)}) collective-permute-start(f32[128,1152]{1,0:T(8,128)} %get-tuple-element.29), channel_id=1, source_target_pairs={{0,8},{8,16},{16,24},{24,32},{32,40},{40,48},{48,56},{56,64},{64,7... | collective-permute-start | bytes 1769480 | tf_op jit(solution)/shard_map/ppermute | solution.py:29
  125.9 5.8 %scatter_fusion.1 = bf16[8,128,1152]{2,1,0:T(8,128)(2,1)} fusion(bf16[8,128,1152]{2,1,0:T(8,128)(2,1)} %broadcast.125.clone.1, s32[7]{0:T(128)S(1)} %copy-done.44, bf16[7,128,1152]{2,1,0:T(8,128)(2,1)} %bitcast.233), kind=kCustom, calls=%fused_computation.4 | custom fusion | bytes 6193180 | tf_op jit(solution)/shard_map/scatter | solution.py:171
  131.7 4.7 %all-to-all-start.1 = ((bf16[8,128,1152]{2,1,0:T(8,128)(2,1)}), bf16[8,128,1152]{2,1,0:T(8,128)(2,1)}, u32[]{:S(2)}, u32[]{:S(2)}) async-start(bf16[8,128,1152]{2,1,0:T(8,128)(2,1)} %scatter_fusion.1), calls=%async_computation.1 | async-start | bytes 4718592 | tf_op jit(solution)/shard_map/all_to_all | solution.py:174
  136.4 3.9 %gather_fusion.2 = bf16[7,128,1152]{2,1,0:T(8,128)(2,1)} fusion(bf16[8,128,1152]{2,1,0:T(8,128)(2,1)} %bitcast.264, s32[1024]{0:T(1024)} %pad_clamp_fusion), kind=kCustom, calls=%fused_computation.2 | custom fusion | bytes 4128796 | tf_op jit(solution)/shard_map/gather | solution.py:113
  142.4 3.6 fusion.100
  149.2 2.5 fusion.28
  157.1 2.5 fusion.29
  165.1 2.5 fusion.30
  171.6 2.5 fusion.31
  176.7 6.4 %pad_maximum_fusion.2 = bf16[2,64,1152]{1,0,2:T(2,128)(2,1)S(1)} fusion(bf16[2,64,288]{1,0,2:T(2,128)(2,1)S(1)} %concatenate.48, bf16[2,64,288]{1,0,2:T(2,128)(2,1)S(1)} %concatenate.47, bf16[2,64,288]{1,0,2:T(2,128)(2,1)} %concatenate.46, bf16[2,64,288]{1,0,2:T(2,128)(2,1)} %concatenate.45), kind=kLoop, calls=%fused_computation.135 | loop fusion | flops 442368 | bytes 589824 | tf_op jit(solution)/shard_map/concatenate | solution.py:148
  184.5 2.9 convolution_multiply_fusion.7
  189.3 3.4 convolution_multiply_fusion.6
  192.7 2.8 copy.80
  195.5 3.3 convolution_multiply_fusion.5
  198.8 2.8 copy.81
  201.6 3.4 convolution_multiply_fusion.4
  205.0 2.7 copy.82
  207.7 8.5 %concatenate.50 = f32[1280,1152]{1,0:T(8,128)} concatenate(f32[1280,288]{1,0:T(8,128)S(1)} %copy.79, f32[1280,288]{1,0:T(8,128)} %copy.80, f32[1280,288]{1,0:T(8,128)} %copy.81, f32[1280,288]{1,0:T(8,128)} %copy.82), dimensions={1} | concatenate | bytes 11796480 | tf_op jit(solution)/shard_map/concatenate | solution.py:149
  216.3 2.4 slice.405
  218.6 2.3 fusion.99
  221.0 5.1 %collective-permute-start.9 = (f32[128,1152]{1,0:T(8,128)}, f32[128,1152]{1,0:T(8,128)}, u32[]{:S(2)}, u32[]{:S(2)}) collective-permute-start(f32[128,1152]{1,0:T(8,128)} %get-tuple-element.31), channel_id=1, source_target_pairs={{0,8},{8,16},{16,24},{24,32},{32,40},{40,48},{48,56},{56,64},{64,7... | collective-permute-start | bytes 1769480 | tf_op jit(solution)/shard_map/ppermute | solution.py:29
  229.1 5.1 %scatter_fusion = bf16[8,128,1152]{2,1,0:T(8,128)(2,1)} fusion(bf16[8,128,1152]{2,1,0:T(8,128)(2,1)} %broadcast.125.clone, s32[7]{0:T(128)S(1)} %copy-done.45, bf16[7,128,1152]{2,1,0:T(8,128)(2,1)S(1)} %bitcast.232), kind=kCustom, calls=%fused_computation.3 | custom fusion | bytes 6193180 | tf_op jit(solution)/shard_map/scatter | solution.py:170
  234.3 5.2 %all-to-all-start = ((bf16[8,128,1152]{2,1,0:T(8,128)(2,1)}), bf16[8,128,1152]{2,1,0:T(8,128)(2,1)}, u32[]{:S(2)}, u32[]{:S(2)}) async-start(bf16[8,128,1152]{2,1,0:T(8,128)(2,1)} %scatter_fusion), calls=%async_computation | async-start | bytes 4718592 | tf_op jit(solution)/shard_map/all_to_all | solution.py:173
  239.4 3.3 fusion.32
  245.6 5.6 %collective-permute-start.12 = (bf16[1,64,1152]{2,1,0:T(8,128)(2,1)S(1)}, bf16[1,64,1152]{2,1,0:T(8,128)(2,1)S(1)}, u32[]{:S(2)}, u32[]{:S(2)}) collective-permute-start(bf16[1,64,1152]{2,1,0:T(8,128)(2,1)S(1)} %get-tuple-element.44), channel_id=1, source_target_pairs={{0,8},{8,16},{16,24},{24,32},{32,40},{40,48},{48,56},{56,64},{64,7... | collective-permute-start | bytes 442376 | tf_op jit(solution)/shard_map/ppermute | solution.py:18
  252.0 94.0 %psum.7 = f32[3,3,1152]{2,1,0:T(4,128)} all-reduce(f32[3,3,1152]{2,1,0:T(4,128)S(1)} %pad_maximum_fusion.3), channel_id=1, replica_groups=mesh['trow'=32,'tcol'=8] {'trow','tcol'}, use_global_device_ids=true, to_apply=%region_23.24 | all-reduce | flops 10368 | bytes 82944 | tf_op jit(solution)/shard_map/psum | solution.py:209
  346.0 2.6 collective-permute-start.15
  348.6 3.0 collective-permute-start.14
  351.6 3.3 fusion.34
  355.0 2.3 fusion.79
  (209 shorter events, 81.1 us)
Async XLA Ops:
  7.2 16.1 %copy-start.14 = (bf16[2,64,1152]{2,1,0:T(8,128)(2,1)S(1)}, bf16[2,64,1152]{2,1,0:T(8,128)(2,1)}, u32[]{:S(2)}) copy-start(bf16[2,64,1152]{2,1,0:T(8,128)(2,1)} %param.10) | copy-start | bytes 884740
  7.2 15.1 %copy-start.17 = (bf16[2,64,1152]{2,1,0:T(8,128)(2,1)S(1)}, bf16[2,64,1152]{2,1,0:T(8,128)(2,1)}, u32[]{:S(2)}) copy-start(bf16[2,64,1152]{2,1,0:T(8,128)(2,1)} %param.7) | copy-start | bytes 884740
  7.2 15.8 %copy-start.41 = (f32[3,3,1152]{2,1,0:T(4,128)S(1)}, f32[3,3,1152]{2,1,0:T(4,128)}, u32[]{:S(2)}) copy-start(f32[3,3,1152]{2,1,0:T(4,128)} %param.11) | copy-start | bytes 124420
  7.2 39.3 %all-gather.3.cloned.1.call-start = ((), (), s32[]{:S(2)}) async-start(), calls=%async_computation.2 | async-start | bytes 2654208 | tf_op jit(solution)/shard_map/all_gather | solution.py:108
  7.9 128.5 %all-gather.5.cloned.1.call-start = ((), (), s32[]{:S(2)}) async-start(), calls=%async_computation.3 | async-start | bytes 2654208 | tf_op jit(solution)/shard_map/all_gather | solution.py:109
  8.0 41.2 %collective-permute-start.1 = (bf16[128,1152]{1,0:T(8,128)(2,1)}, bf16[128,1152]{1,0:T(8,128)(2,1)}, u32[]{:S(2)}, u32[]{:S(2)}) collective-permute-start(bf16[128,1152]{1,0:T(8,128)(2,1)} %bitcast.266), channel_id=1, source_target_pairs={{8,0},{16,8},{24,16},{32,24},{40,32},{48,40},{56,48},{64,56},{72,6... | collective-permute-start | bytes 884744 | tf_op jit(solution)/shard_map/ppermute | solution.py:29
  9.3 39.9 %collective-permute-start = (bf16[128,1152]{1,0:T(8,128)(2,1)}, bf16[128,1152]{1,0:T(8,128)(2,1)}, u32[]{:S(2)}, u32[]{:S(2)}) collective-permute-start(bf16[128,1152]{1,0:T(8,128)(2,1)} %bitcast.267), channel_id=1, source_target_pairs={{0,8},{8,16},{16,24},{24,32},{32,40},{40,48},{48,56},{56,64},{64,7... | collective-permute-start | bytes 884744 | tf_op jit(solution)/shard_map/ppermute | solution.py:29
  15.6 7.6 %collective-permute-start.2 = (bf16[1,64,1152]{2,1,0:T(8,128)(2,1)S(1)}, bf16[1,64,1152]{2,1,0:T(8,128)(2,1)S(1)}, u32[]{:S(2)}, u32[]{:S(2)}) collective-permute-start(bf16[1,64,1152]{2,1,0:T(8,128)(2,1)S(1)} %get-tuple-element.55), channel_id=1, source_target_pairs={{0,8},{8,16},{16,24},{24,32},{32,40},{40,48},{48,56},{56,64},{64,7... | collective-permute-start | bytes 442376 | tf_op jit(solution)/shard_map/ppermute | solution.py:18
  18.2 5.9 %collective-permute-start.3 = (bf16[1,64,1152]{2,1,0:T(8,128)(2,1)S(1)}, bf16[1,64,1152]{2,1,0:T(8,128)(2,1)S(1)}, u32[]{:S(2)}, u32[]{:S(2)}) collective-permute-start(bf16[1,64,1152]{2,1,0:T(8,128)(2,1)S(1)} %get-tuple-element.54), channel_id=1, source_target_pairs={{8,0},{16,8},{24,16},{32,24},{40,32},{48,40},{56,48},{64,56},{72,6... | collective-permute-start | bytes 442376 | tf_op jit(solution)/shard_map/ppermute | solution.py:21
  20.3 17.0 %copy-start.46 = (s32[1,8,8]{2,1,0:T(8,128)S(1)}, s32[1,8,8]{2,1,0:T(8,128)}, u32[]{:S(2)}) copy-start(s32[1,8,8]{2,1,0:T(8,128)} %param.13) | copy-start | bytes 772
  23.0 15.1 %copy-start.18 = (bf16[2,64,1152]{2,1,0:T(8,128)(2,1)S(1)}, bf16[2,64,1152]{2,1,0:T(8,128)(2,1)}, u32[]{:S(2)}) copy-start(bf16[2,64,1152]{2,1,0:T(8,128)(2,1)} %param.9) | copy-start | bytes 884740
  23.1 16.2 %copy-start.27 = (f32[1152]{0:T(1024)}, f32[1152]{0:T(1024)S(1)}, u32[]{:S(2)}) copy-start(f32[1152]{0:T(1024)S(1)} %get-tuple-element.21) | copy-start | bytes 13828
  23.1 16.2 %copy-start.29 = (f32[1152]{0:T(1024)}, f32[1152]{0:T(1024)S(1)}, u32[]{:S(2)}) copy-start(f32[1152]{0:T(1024)S(1)} %get-tuple-element.22) | copy-start | bytes 13828
  23.2 16.2 %copy-start.31 = (f32[1152]{0:T(1024)}, f32[1152]{0:T(1024)S(1)}, u32[]{:S(2)}) copy-start(f32[1152]{0:T(1024)S(1)} %get-tuple-element.23) | copy-start | bytes 13828
  23.2 16.2 %copy-start.33 = (f32[1152]{0:T(1024)}, f32[1152]{0:T(1024)S(1)}, u32[]{:S(2)}) copy-start(f32[1152]{0:T(1024)S(1)} %get-tuple-element.24) | copy-start | bytes 13828
  23.2 16.2 %copy-start.35 = (f32[1152]{0:T(1024)}, f32[1152]{0:T(1024)S(1)}, u32[]{:S(2)}) copy-start(f32[1152]{0:T(1024)S(1)} %get-tuple-element.25) | copy-start | bytes 13828
  23.2 16.2 %copy-start.37 = (f32[1152]{0:T(1024)}, f32[1152]{0:T(1024)S(1)}, u32[]{:S(2)}) copy-start(f32[1152]{0:T(1024)S(1)} %get-tuple-element.26) | copy-start | bytes 13828
  23.2 16.2 %copy-start.39 = (f32[1152]{0:T(1024)}, f32[1152]{0:T(1024)S(1)}, u32[]{:S(2)}) copy-start(f32[1152]{0:T(1024)S(1)} %get-tuple-element.27) | copy-start | bytes 13828
  24.2 13.7 %collective-permute-start.5 = (bf16[4,1,1152]{2,1,0:T(2,128)(2,1)S(1)}, bf16[4,1,1152]{2,1,0:T(2,128)(2,1)S(1)}, u32[]{:S(2)}, u32[]{:S(2)}) collective-permute-start(bf16[4,1,1152]{2,1,0:T(2,128)(2,1)S(1)} %get-tuple-element.43), channel_id=1, source_target_pairs={{1,0},{2,1},{3,2},{4,3},{5,4},{6,5},{7,6},{9,8},{10,9},{11,10},{12... | collective-permute-start | bytes 27656 | tf_op jit(solution)/shard_map/ppermute | solution.py:21
  29.1 8.8 %collective-permute-start.4 = (bf16[4,1,1152]{2,1,0:T(2,128)(2,1)S(1)}, bf16[4,1,1152]{2,1,0:T(2,128)(2,1)S(1)}, u32[]{:S(2)}, u32[]{:S(2)}) collective-permute-start(bf16[4,1,1152]{2,1,0:T(2,128)(2,1)S(1)} %get-tuple-element.42), channel_id=1, source_target_pairs={{0,1},{1,2},{2,3},{3,4},{4,5},{5,6},{6,7},{8,9},{9,10},{10,11},{11... | collective-permute-start | bytes 27656 | tf_op jit(solution)/shard_map/ppermute | solution.py:18
  39.4 101.0 %collective-permute-start.7 = (bf16[128,1152]{1,0:T(8,128)(2,1)}, bf16[128,1152]{1,0:T(8,128)(2,1)}, u32[]{:S(2)}, u32[]{:S(2)}) collective-permute-start(bf16[128,1152]{1,0:T(8,128)(2,1)} %bitcast.12), channel_id=1, source_target_pairs={{8,0},{16,8},{24,16},{32,24},{40,32},{48,40},{56,48},{64,56},{72,6... | collective-permute-start | bytes 884744 | tf_op jit(solution)/shard_map/ppermute | solution.py:29
  40.7 99.7 %collective-permute-start.6 = (bf16[128,1152]{1,0:T(8,128)(2,1)}, bf16[128,1152]{1,0:T(8,128)(2,1)}, u32[]{:S(2)}, u32[]{:S(2)}) collective-permute-start(bf16[128,1152]{1,0:T(8,128)(2,1)} %bitcast.12), channel_id=1, source_target_pairs={{0,8},{8,16},{16,24},{24,32},{32,40},{40,48},{48,56},{56,64},{64,7... | collective-permute-start | bytes 884744 | tf_op jit(solution)/shard_map/ppermute | solution.py:29
  55.8 4.1 %copy-start.7 = (bf16[1280,288]{0,1:T(8,128)(2,1)}, bf16[1280,288]{0,1:T(8,128)(2,1)S(1)}, u32[]{:S(2)}) copy-start(bf16[1280,288]{0,1:T(8,128)(2,1)S(1)} %copy.51) | copy-start | bytes 2211844
  55.9 4.0 %copy-start.26 = (bf16[128,288]{0,1:T(8,128)(2,1)S(1)}, bf16[128,288]{0,1:T(8,128)(2,1)}, u32[]{:S(2)}) copy-start(bf16[128,288]{0,1:T(8,128)(2,1)} %copy.112) | copy-start | bytes 221188
  70.3 11.0 %copy-start.10 = (bf16[1280,288]{0,1:T(8,128)(2,1)}, bf16[1280,288]{0,1:T(8,128)(2,1)S(1)}, u32[]{:S(2)}) copy-start(bf16[1280,288]{0,1:T(8,128)(2,1)S(1)} %copy.63) | copy-start | bytes 2211844
  84.9 3.1 copy-start.15
  90.0 2.9 copy-start.12
  96.4 3.0 copy-start.16
  116.8 9.1 %copy-start.44 = (s32[7]{0:T(128)S(1)}, s32[7]{0:T(128)}, u32[]{:S(2)}) copy-start(s32[7]{0:T(128)} %copy-done.43) | copy-start | bytes 88
  119.2 123.5 %collective-permute-start.11 = (f32[128,1152]{1,0:T(8,128)}, f32[128,1152]{1,0:T(8,128)}, u32[]{:S(2)}, u32[]{:S(2)}) collective-permute-start(f32[128,1152]{1,0:T(8,128)} %get-tuple-element.29), channel_id=1, source_target_pairs={{0,8},{8,16},{16,24},{24,32},{32,40},{40,48},{48,56},{56,64},{64,7... | collective-permute-start | bytes 1769480 | tf_op jit(solution)/shard_map/ppermute | solution.py:29
  122.9 119.8 %collective-permute-start.10 = (f32[128,1152]{1,0:T(8,128)}, f32[128,1152]{1,0:T(8,128)}, u32[]{:S(2)}, u32[]{:S(2)}) collective-permute-start(f32[128,1152]{1,0:T(8,128)} %get-tuple-element.28), channel_id=1, source_target_pairs={{8,0},{16,8},{24,16},{32,24},{40,32},{48,40},{56,48},{64,56},{72,6... | collective-permute-start | bytes 1769480 | tf_op jit(solution)/shard_map/ppermute | solution.py:29
  131.7 102.5 %all-to-all-start.1 = ((bf16[8,128,1152]{2,1,0:T(8,128)(2,1)}), bf16[8,128,1152]{2,1,0:T(8,128)(2,1)}, u32[]{:S(2)}, u32[]{:S(2)}) async-start(bf16[8,128,1152]{2,1,0:T(8,128)(2,1)} %scatter_fusion.1), calls=%async_computation.1 | async-start | bytes 4718592 | tf_op jit(solution)/shard_map/all_to_all | solution.py:174
  149.2 3.6 copy-start.13
  157.1 3.7 %copy-start.11 = (bf16[1280,288]{0,1:T(8,128)(2,1)S(1)}, bf16[1280,288]{0,1:T(8,128)(2,1)}, u32[]{:S(2)}) copy-start(bf16[1280,288]{0,1:T(8,128)(2,1)} %copy-done.10) | copy-start | bytes 2211844
  165.0 3.6 copy-start.9
  171.6 3.0 copy-start.19
  192.6 2.8 copy-start.23
  198.8 2.8 copy-start.22
  218.6 10.5 %copy-start.45 = (s32[7]{0:T(128)S(1)}, s32[7]{0:T(128)}, u32[]{:S(2)}) copy-start(s32[7]{0:T(128)} %copy-done.43) | copy-start | bytes 88
  221.0 134.0 %collective-permute-start.9 = (f32[128,1152]{1,0:T(8,128)}, f32[128,1152]{1,0:T(8,128)}, u32[]{:S(2)}, u32[]{:S(2)}) collective-permute-start(f32[128,1152]{1,0:T(8,128)} %get-tuple-element.31), channel_id=1, source_target_pairs={{0,8},{8,16},{16,24},{24,32},{32,40},{40,48},{48,56},{56,64},{64,7... | collective-permute-start | bytes 1769480 | tf_op jit(solution)/shard_map/ppermute | solution.py:29
  226.1 128.9 %collective-permute-start.8 = (f32[128,1152]{1,0:T(8,128)}, f32[128,1152]{1,0:T(8,128)}, u32[]{:S(2)}, u32[]{:S(2)}) collective-permute-start(f32[128,1152]{1,0:T(8,128)} %get-tuple-element.30), channel_id=1, source_target_pairs={{8,0},{16,8},{24,16},{32,24},{40,32},{48,40},{56,48},{64,56},{72,6... | collective-permute-start | bytes 1769480 | tf_op jit(solution)/shard_map/ppermute | solution.py:29
  234.3 5.2 %copy-start.42 = (pred[8]{0:T(512)(128)(4,1)S(1)}, pred[8]{0:T(512)(128)(4,1)}, u32[]{:S(2)}) copy-start(pred[8]{0:T(512)(128)(4,1)} %fusion.80) | copy-start | bytes 28
  234.3 117.4 %all-to-all-start = ((bf16[8,128,1152]{2,1,0:T(8,128)(2,1)}), bf16[8,128,1152]{2,1,0:T(8,128)(2,1)}, u32[]{:S(2)}, u32[]{:S(2)}) async-start(bf16[8,128,1152]{2,1,0:T(8,128)(2,1)} %scatter_fusion), calls=%async_computation | async-start | bytes 4718592 | tf_op jit(solution)/shard_map/all_to_all | solution.py:173
  244.2 113.0 %copy-start.3 = (bf16[128,1152]{1,0:T(8,128)(2,1)}, bf16[128,1152]{1,0:T(8,128)(2,1)S(1)}, u32[]{:S(2)}) copy-start(bf16[128,1152]{1,0:T(8,128)(2,1)S(1)} %fusion.76) | copy-start | bytes 884740
  244.3 101.7 %collective-permute-start.13 = (bf16[1,64,1152]{2,1,0:T(8,128)(2,1)S(1)}, bf16[1,64,1152]{2,1,0:T(8,128)(2,1)S(1)}, u32[]{:S(2)}, u32[]{:S(2)}) collective-permute-start(bf16[1,64,1152]{2,1,0:T(8,128)(2,1)S(1)} %get-tuple-element.45), channel_id=1, source_target_pairs={{8,0},{16,8},{24,16},{32,24},{40,32},{48,40},{56,48},{64,56},{72,6... | collective-permute-start | bytes 442376 | tf_op jit(solution)/shard_map/ppermute | solution.py:21
  245.6 100.4 %collective-permute-start.12 = (bf16[1,64,1152]{2,1,0:T(8,128)(2,1)S(1)}, bf16[1,64,1152]{2,1,0:T(8,128)(2,1)S(1)}, u32[]{:S(2)}, u32[]{:S(2)}) collective-permute-start(bf16[1,64,1152]{2,1,0:T(8,128)(2,1)S(1)} %get-tuple-element.44), channel_id=1, source_target_pairs={{0,8},{8,16},{16,24},{24,32},{32,40},{40,48},{48,56},{56,64},{64,7... | collective-permute-start | bytes 442376 | tf_op jit(solution)/shard_map/ppermute | solution.py:18
  346.0 11.2 %collective-permute-start.15 = (bf16[4,1,1152]{2,1,0:T(2,128)(2,1)S(1)}, bf16[4,1,1152]{2,1,0:T(2,128)(2,1)S(1)}, u32[]{:S(2)}, u32[]{:S(2)}) collective-permute-start(bf16[4,1,1152]{2,1,0:T(2,128)(2,1)S(1)} %get-tuple-element.41), channel_id=1, source_target_pairs={{1,0},{2,1},{3,2},{4,3},{5,4},{6,5},{7,6},{9,8},{10,9},{11,10},{12... | collective-permute-start | bytes 27656 | tf_op jit(solution)/shard_map/ppermute | solution.py:21
  348.6 8.6 %collective-permute-start.14 = (bf16[4,1,1152]{2,1,0:T(2,128)(2,1)S(1)}, bf16[4,1,1152]{2,1,0:T(2,128)(2,1)S(1)}, u32[]{:S(2)}, u32[]{:S(2)}) collective-permute-start(bf16[4,1,1152]{2,1,0:T(2,128)(2,1)S(1)} %get-tuple-element.40), channel_id=1, source_target_pairs={{0,1},{1,2},{2,3},{3,4},{4,5},{5,6},{6,7},{8,9},{9,10},{10,11},{11... | collective-permute-start | bytes 27656 | tf_op jit(solution)/shard_map/ppermute | solution.py:18
  (20 other events, 36.6 us)
Sparse Core Ops, SparseCore 0:
  9.8 32.3 all-gather.2
  46.6 34.6 all-gather.4
where the time goes:
time: 373 us; the launch traced here: 366 us
  local copies, waits for them, and re-layouts  108 us (29%)
  blocking collectives  94 us (25%)
  matrix products  60.8 us (16%)
  starting transfers between devices  59 us (16%)
  other arithmetic  26.9 us (7%)
  between operations  15.3 us (4%)
    psum x1, blocking collectives, per_device(): grad_kernel = lax.psum(jnp.stack(kernel_rows, axis=0), ('trow', 'tcol'))  94 us
    ppermute x8, starting transfers between devices, from_behind(): return lax.ppermute(shard, axis, pairs)  25 us
    ppermute x4, starting transfers between devices, with_halo(): lax.ppermute(lax.slice_in_dim(block, block.shape[dim] - width, None, axis...  14 us
    sub x4, matrix products, attend_group(): raised = jnp.exp(scores - row_top)  13.8 us
    unnamed x107, local copies, waits for them, and re-layouts  13.1 us
    dot_general x4, matrix products, attend_group(): jnp.einsum('hqk,qhd->khd', grad_scores_bf, queries, preferred_element_typ...  13 us
    reshape x4, local copies, waits for them, and re-layouts, per_device(): value_parts.append(grad_v.reshape(-1, col_span))  11.4 us
    reshape x4, local copies, waits for them, and re-layouts, per_device(): key_parts.append(grad_k.reshape(-1, col_span))  10.2 us
  transfers between devices with their start and end apart: 20, of which 1 were waited for; matrix products, arithmetic and copies ran while one was open for 51% of the time, Pallas kernels for 0%

commit v1 on v0

--- a/solution.py
+++ b/solution.py
@@ -206,7 +206,9 @@
                 )
             )
         kernel_rows.append(jnp.stack(kernel_cols, axis=0))
-    grad_kernel = lax.psum(jnp.stack(kernel_rows, axis=0), ("trow", "tcol"))
+    grad_kernel = jnp.stack(kernel_rows, axis=0)
+    for over in ("trow", "tcol"):
+        grad_kernel = lax.psum(grad_kernel, over)
     grad_query = query_gradient_total.astype(jnp.bfloat16).reshape(
         tile_rows, tile_column_count, channels
     )

time: 373 us -> 451 us (1.21)
  the two profiles are of different devices: /device:TPU:1 before, /device:TPU:129 now
where the time goes in v1:
time: 451 us; the launch traced here: 444 us
  blocking collectives  163 us (36%)
  local copies, waits for them, and re-layouts  108 us (24%)
  starting transfers between devices  68.2 us (15%)
  matrix products  60.8 us (13%)
  other arithmetic  26.8 us (6%)
  between operations  15.3 us (3%)
    psum x2, blocking collectives, per_device(): grad_kernel = lax.psum(grad_kernel, over)  163 us
    ppermute x8, starting transfers between devices, from_behind(): return lax.ppermute(shard, axis, pairs)  30.1 us
    ppermute x4, starting transfers between devices, with_halo(): lax.ppermute(lax.slice_in_dim(block, 0, width, axis=dim), axis, backward)  16.7 us
    sub x4, matrix products, attend_group(): raised = jnp.exp(scores - row_top)  13.8 us
    unnamed x107, local copies, waits for them, and re-layouts  13.1 us
    dot_general x4, matrix products, attend_group(): jnp.einsum('hqk,qhd->khd', grad_scores_bf, queries, preferred_element_typ...  13 us
    reshape x4, local copies, waits for them, and re-layouts, per_device(): value_parts.append(grad_v.reshape(-1, col_span))  11.4 us
    ppermute x4, starting transfers between devices, with_halo(): lax.ppermute(lax.slice_in_dim(block, block.shape[dim] - width, None, axis...  10.9 us
  transfers between devices with their start and end apart: 20, of which 1 were waited for; matrix products, arithmetic and copies ran while one was open for 42% of the time, Pallas kernels for 0%

profile of v1, /device:TPU:129, one launch (start us, length us, event | category | flops | bytes accessed | tf_op | source)
XLA Modules:
  0.0 444.5 jit_solution(10878431707300282132)
XLA Ops:
  8.0 3.9 collective-permute-start.1
  14.9 2.5 collective-permute-start.2
  17.4 6.1 %collective-permute-start.3 = (bf16[1,64,1152]{2,1,0:T(8,128)(2,1)S(1)}, bf16[1,64,1152]{2,1,0:T(8,128)(2,1)S(1)}, u32[]{:S(2)}, u32[]{:S(2)}) collective-permute-start(bf16[1,64,1152]{2,1,0:T(8,128)(2,1)S(1)} %get-tuple-element.54), channel_id=1, source_target_pairs={{8,0},{16,8},{24,16},{32,24},{40,32},{48,40},{56,48},{64,56},{72,6... | collective-permute-start | bytes 442376 | tf_op jit(solution)/shard_map/ppermute | solution.py:21
  28.3 3.7 collective-permute-start.5
  32.0 3.1 collective-permute-start.4
  42.6 5.1 %collective-permute-start.7 = (bf16[128,1152]{1,0:T(8,128)(2,1)}, bf16[128,1152]{1,0:T(8,128)(2,1)}, u32[]{:S(2)}, u32[]{:S(2)}) collective-permute-start(bf16[128,1152]{1,0:T(8,128)(2,1)} %bitcast.12), channel_id=1, source_target_pairs={{8,0},{16,8},{24,16},{32,24},{40,32},{48,40},{56,48},{64,56},{72,6... | collective-permute-start | bytes 884744 | tf_op jit(solution)/shard_map/ppermute | solution.py:29
  49.7 2.7 gather_fusion.1
  53.7 3.0 fusion.101
  59.0 4.0 fusion.108
  63.1 2.7 fusion.109
  73.5 3.0 copy.87
  81.6 2.7 copy.88
  84.4 3.6 fusion.107
  93.1 2.8 copy.89
  96.0 3.5 fusion.106
  104.6 2.8 copy.90
  107.4 8.9 %concatenate.51 = f32[1280,1152]{1,0:T(8,128)} concatenate(f32[1280,288]{1,0:T(8,128)} %copy.87, f32[1280,288]{1,0:T(8,128)} %copy.88, f32[1280,288]{1,0:T(8,128)} %copy.89, f32[1280,288]{1,0:T(8,128)} %copy.90), dimensions={1} | concatenate | bytes 11796480 | tf_op jit(solution)/shard_map/concatenate | solution.py:150
  116.2 3.7 slice.404
  119.9 2.4 fusion.98
  124.2 6.7 %collective-permute-start.10 = (f32[128,1152]{1,0:T(8,128)}, f32[128,1152]{1,0:T(8,128)}, u32[]{:S(2)}, u32[]{:S(2)}) collective-permute-start(f32[128,1152]{1,0:T(8,128)} %get-tuple-element.28), channel_id=1, source_target_pairs={{8,0},{16,8},{24,16},{32,24},{40,32},{48,40},{56,48},{64,56},{72,6... | collective-permute-start | bytes 1769480 | tf_op jit(solution)/shard_map/ppermute | solution.py:29
  132.7 5.8 %scatter_fusion.1 = bf16[8,128,1152]{2,1,0:T(8,128)(2,1)} fusion(bf16[8,128,1152]{2,1,0:T(8,128)(2,1)} %broadcast.125.clone.1, s32[7]{0:T(128)S(1)} %copy-done.44, bf16[7,128,1152]{2,1,0:T(8,128)(2,1)} %bitcast.233), kind=kCustom, calls=%fused_computation.4 | custom fusion | bytes 6193180 | tf_op jit(solution)/shard_map/scatter | solution.py:171
  138.5 4.9 %all-to-all-start.1 = ((bf16[8,128,1152]{2,1,0:T(8,128)(2,1)}), bf16[8,128,1152]{2,1,0:T(8,128)(2,1)}, u32[]{:S(2)}, u32[]{:S(2)}) async-start(bf16[8,128,1152]{2,1,0:T(8,128)(2,1)} %scatter_fusion.1), calls=%async_computation.1 | async-start | bytes 4718592 | tf_op jit(solution)/shard_map/all_to_all | solution.py:174
  143.4 3.9 gather_fusion.2
  149.4 3.6 fusion.100
  156.2 2.5 fusion.28
  164.1 2.5 fusion.29
  172.0 2.5 fusion.30
  178.6 2.5 fusion.31
  183.7 6.4 %pad_maximum_fusion.2 = bf16[2,64,1152]{1,0,2:T(2,128)(2,1)S(1)} fusion(bf16[2,64,288]{1,0,2:T(2,128)(2,1)S(1)} %concatenate.48, bf16[2,64,288]{1,0,2:T(2,128)(2,1)S(1)} %concatenate.47, bf16[2,64,288]{1,0,2:T(2,128)(2,1)} %concatenate.46, bf16[2,64,288]{1,0,2:T(2,128)(2,1)} %concatenate.45), kind=kLoop, calls=%fused_computation.135 | loop fusion | flops 442368 | bytes 589824 | tf_op jit(solution)/shard_map/concatenate | solution.py:148
  191.5 2.9 convolution_multiply_fusion.7
  196.3 3.4 convolution_multiply_fusion.6
  199.6 2.8 copy.80
  202.4 3.3 convolution_multiply_fusion.5
  205.8 2.8 copy.81
  208.6 3.4 convolution_multiply_fusion.4
  211.9 2.7 copy.82
  214.7 8.5 %concatenate.50 = f32[1280,1152]{1,0:T(8,128)} concatenate(f32[1280,288]{1,0:T(8,128)S(1)} %copy.79, f32[1280,288]{1,0:T(8,128)} %copy.80, f32[1280,288]{1,0:T(8,128)} %copy.81, f32[1280,288]{1,0:T(8,128)} %copy.82), dimensions={1} | concatenate | bytes 11796480 | tf_op jit(solution)/shard_map/concatenate | solution.py:149
  223.2 2.4 slice.405
  225.6 2.3 fusion.99
  229.9 6.7 %collective-permute-start.8 = (f32[128,1152]{1,0:T(8,128)}, f32[128,1152]{1,0:T(8,128)}, u32[]{:S(2)}, u32[]{:S(2)}) collective-permute-start(f32[128,1152]{1,0:T(8,128)} %get-tuple-element.30), channel_id=1, source_target_pairs={{8,0},{16,8},{24,16},{32,24},{40,32},{48,40},{56,48},{64,56},{72,6... | collective-permute-start | bytes 1769480 | tf_op jit(solution)/shard_map/ppermute | solution.py:29
  238.4 5.1 %scatter_fusion = bf16[8,128,1152]{2,1,0:T(8,128)(2,1)} fusion(bf16[8,128,1152]{2,1,0:T(8,128)(2,1)} %broadcast.125.clone, s32[7]{0:T(128)S(1)} %copy-done.45, bf16[7,128,1152]{2,1,0:T(8,128)(2,1)S(1)} %bitcast.232), kind=kCustom, calls=%fused_computation.3 | custom fusion | bytes 6193180 | tf_op jit(solution)/shard_map/scatter | solution.py:170
  243.5 5.5 %all-to-all-start = ((bf16[8,128,1152]{2,1,0:T(8,128)(2,1)}), bf16[8,128,1152]{2,1,0:T(8,128)(2,1)}, u32[]{:S(2)}, u32[]{:S(2)}) async-start(bf16[8,128,1152]{2,1,0:T(8,128)(2,1)} %scatter_fusion), calls=%async_computation | async-start | bytes 4718592 | tf_op jit(solution)/shard_map/all_to_all | solution.py:173
  248.9 3.3 fusion.32
  255.7 3.4 collective-permute-start.12
  259.9 113.6 %psum.14 = f32[3,3,1152]{2,1,0:T(4,128)S(1)} all-reduce(f32[3,3,1152]{2,1,0:T(4,128)S(1)} %pad_maximum_fusion.3), channel_id=1, replica_groups=mesh['trow'=32,'tcol'=8] {'trow'}, use_global_device_ids=true, to_apply=%region_23.24 | all-reduce | flops 10368 | bytes 82944 | tf_op jit(solution)/shard_map/psum | solution.py:211
  373.4 49.9 %psum.15 = f32[3,3,1152]{2,1,0:T(4,128)} all-reduce(f32[3,3,1152]{2,1,0:T(4,128)S(1)} %psum.14), channel_id=1, replica_groups=mesh['trow'=32,'tcol'=8] {'tcol'}, use_global_device_ids=true, to_apply=%region_24.25 | all-reduce | flops 10368 | bytes 82944 | tf_op jit(solution)/shard_map/psum | solution.py:211
  423.3 5.0 %collective-permute-start.15 = (bf16[4,1,1152]{2,1,0:T(2,128)(2,1)S(1)}, bf16[4,1,1152]{2,1,0:T(2,128)(2,1)S(1)}, u32[]{:S(2)}, u32[]{:S(2)}) collective-permute-start(bf16[4,1,1152]{2,1,0:T(2,128)(2,1)S(1)} %get-tuple-element.41), channel_id=1, source_target_pairs={{1,0},{2,1},{3,2},{4,3},{5,4},{6,5},{7,6},{9,8},{10,9},{11,10},{12... | collective-permute-start | bytes 27656 | tf_op jit(solution)/shard_map/ppermute | solution.py:21
  430.3 3.3 fusion.34
  (210 shorter events, 87.2 us)
Async XLA Ops:
  7.2 21.0 %copy-start.14 = (bf16[2,64,1152]{2,1,0:T(8,128)(2,1)S(1)}, bf16[2,64,1152]{2,1,0:T(8,128)(2,1)}, u32[]{:S(2)}) copy-start(bf16[2,64,1152]{2,1,0:T(8,128)(2,1)} %param.10) | copy-start | bytes 884740
  7.2 19.0 %copy-start.17 = (bf16[2,64,1152]{2,1,0:T(8,128)(2,1)S(1)}, bf16[2,64,1152]{2,1,0:T(8,128)(2,1)}, u32[]{:S(2)}) copy-start(bf16[2,64,1152]{2,1,0:T(8,128)(2,1)} %param.7) | copy-start | bytes 884740
  7.2 19.8 %copy-start.41 = (f32[3,3,1152]{2,1,0:T(4,128)S(1)}, f32[3,3,1152]{2,1,0:T(4,128)}, u32[]{:S(2)}) copy-start(f32[3,3,1152]{2,1,0:T(4,128)} %param.11) | copy-start | bytes 124420
  7.2 42.5 %all-gather.3.cloned.1.call-start = ((), (), s32[]{:S(2)}) async-start(), calls=%async_computation.2 | async-start | bytes 2654208 | tf_op jit(solution)/shard_map/all_gather | solution.py:108
  7.9 135.5 %all-gather.5.cloned.1.call-start = ((), (), s32[]{:S(2)}) async-start(), calls=%async_computation.3 | async-start | bytes 2654208 | tf_op jit(solution)/shard_map/all_gather | solution.py:109
  8.0 44.4 %collective-permute-start.1 = (bf16[128,1152]{1,0:T(8,128)(2,1)}, bf16[128,1152]{1,0:T(8,128)(2,1)}, u32[]{:S(2)}, u32[]{:S(2)}) collective-permute-start(bf16[128,1152]{1,0:T(8,128)(2,1)} %bitcast.266), channel_id=1, source_target_pairs={{8,0},{16,8},{24,16},{32,24},{40,32},{48,40},{56,48},{64,56},{72,6... | collective-permute-start | bytes 884744 | tf_op jit(solution)/shard_map/ppermute | solution.py:29
  11.9 40.5 %collective-permute-start = (bf16[128,1152]{1,0:T(8,128)(2,1)}, bf16[128,1152]{1,0:T(8,128)(2,1)}, u32[]{:S(2)}, u32[]{:S(2)}) collective-permute-start(bf16[128,1152]{1,0:T(8,128)(2,1)} %bitcast.267), channel_id=1, source_target_pairs={{0,8},{8,16},{16,24},{24,32},{32,40},{40,48},{48,56},{56,64},{64,7... | collective-permute-start | bytes 884744 | tf_op jit(solution)/shard_map/ppermute | solution.py:29
  14.9 13.3 %collective-permute-start.2 = (bf16[1,64,1152]{2,1,0:T(8,128)(2,1)S(1)}, bf16[1,64,1152]{2,1,0:T(8,128)(2,1)S(1)}, u32[]{:S(2)}, u32[]{:S(2)}) collective-permute-start(bf16[1,64,1152]{2,1,0:T(8,128)(2,1)S(1)} %get-tuple-element.55), channel_id=1, source_target_pairs={{0,8},{8,16},{16,24},{24,32},{32,40},{40,48},{48,56},{56,64},{64,7... | collective-permute-start | bytes 442376 | tf_op jit(solution)/shard_map/ppermute | solution.py:18
  17.4 10.8 %collective-permute-start.3 = (bf16[1,64,1152]{2,1,0:T(8,128)(2,1)S(1)}, bf16[1,64,1152]{2,1,0:T(8,128)(2,1)S(1)}, u32[]{:S(2)}, u32[]{:S(2)}) collective-permute-start(bf16[1,64,1152]{2,1,0:T(8,128)(2,1)S(1)} %get-tuple-element.54), channel_id=1, source_target_pairs={{8,0},{16,8},{24,16},{32,24},{40,32},{48,40},{56,48},{64,56},{72,6... | collective-permute-start | bytes 442376 | tf_op jit(solution)/shard_map/ppermute | solution.py:21
  24.2 16.2 %copy-start.46 = (s32[1,8,8]{2,1,0:T(8,128)S(1)}, s32[1,8,8]{2,1,0:T(8,128)}, u32[]{:S(2)}) copy-start(s32[1,8,8]{2,1,0:T(8,128)} %param.13) | copy-start | bytes 772
  27.0 14.4 %copy-start.18 = (bf16[2,64,1152]{2,1,0:T(8,128)(2,1)S(1)}, bf16[2,64,1152]{2,1,0:T(8,128)(2,1)}, u32[]{:S(2)}) copy-start(bf16[2,64,1152]{2,1,0:T(8,128)(2,1)} %param.9) | copy-start | bytes 884740
  27.1 15.5 %copy-start.27 = (f32[1152]{0:T(1024)}, f32[1152]{0:T(1024)S(1)}, u32[]{:S(2)}) copy-start(f32[1152]{0:T(1024)S(1)} %get-tuple-element.21) | copy-start | bytes 13828
  27.1 15.5 %copy-start.29 = (f32[1152]{0:T(1024)}, f32[1152]{0:T(1024)S(1)}, u32[]{:S(2)}) copy-start(f32[1152]{0:T(1024)S(1)} %get-tuple-element.22) | copy-start | bytes 13828
  27.1 15.5 %copy-start.31 = (f32[1152]{0:T(1024)}, f32[1152]{0:T(1024)S(1)}, u32[]{:S(2)}) copy-start(f32[1152]{0:T(1024)S(1)} %get-tuple-element.23) | copy-start | bytes 13828
  27.1 15.5 %copy-start.33 = (f32[1152]{0:T(1024)}, f32[1152]{0:T(1024)S(1)}, u32[]{:S(2)}) copy-start(f32[1152]{0:T(1024)S(1)} %get-tuple-element.24) | copy-start | bytes 13828
  27.1 15.5 %copy-start.35 = (f32[1152]{0:T(1024)}, f32[1152]{0:T(1024)S(1)}, u32[]{:S(2)}) copy-start(f32[1152]{0:T(1024)S(1)} %get-tuple-element.25) | copy-start | bytes 13828
  27.1 15.5 %copy-start.37 = (f32[1152]{0:T(1024)}, f32[1152]{0:T(1024)S(1)}, u32[]{:S(2)}) copy-start(f32[1152]{0:T(1024)S(1)} %get-tuple-element.26) | copy-start | bytes 13828
  27.1 15.5 %copy-start.39 = (f32[1152]{0:T(1024)}, f32[1152]{0:T(1024)S(1)}, u32[]{:S(2)}) copy-start(f32[1152]{0:T(1024)S(1)} %get-tuple-element.27) | copy-start | bytes 13828
  28.3 12.9 %collective-permute-start.5 = (bf16[4,1,1152]{2,1,0:T(2,128)(2,1)S(1)}, bf16[4,1,1152]{2,1,0:T(2,128)(2,1)S(1)}, u32[]{:S(2)}, u32[]{:S(2)}) collective-permute-start(bf16[4,1,1152]{2,1,0:T(2,128)(2,1)S(1)} %get-tuple-element.43), channel_id=1, source_target_pairs={{1,0},{2,1},{3,2},{4,3},{5,4},{6,5},{7,6},{9,8},{10,9},{11,10},{12... | collective-permute-start | bytes 27656 | tf_op jit(solution)/shard_map/ppermute | solution.py:21
  32.0 9.2 %collective-permute-start.4 = (bf16[4,1,1152]{2,1,0:T(2,128)(2,1)S(1)}, bf16[4,1,1152]{2,1,0:T(2,128)(2,1)S(1)}, u32[]{:S(2)}, u32[]{:S(2)}) collective-permute-start(bf16[4,1,1152]{2,1,0:T(2,128)(2,1)S(1)} %get-tuple-element.42), channel_id=1, source_target_pairs={{0,1},{1,2},{2,3},{3,4},{4,5},{5,6},{6,7},{8,9},{9,10},{10,11},{11... | collective-permute-start | bytes 27656 | tf_op jit(solution)/shard_map/ppermute | solution.py:18
  42.6 104.8 %collective-permute-start.7 = (bf16[128,1152]{1,0:T(8,128)(2,1)}, bf16[128,1152]{1,0:T(8,128)(2,1)}, u32[]{:S(2)}, u32[]{:S(2)}) collective-permute-start(bf16[128,1152]{1,0:T(8,128)(2,1)} %bitcast.12), channel_id=1, source_target_pairs={{8,0},{16,8},{24,16},{32,24},{40,32},{48,40},{56,48},{64,56},{72,6... | collective-permute-start | bytes 884744 | tf_op jit(solution)/shard_map/ppermute | solution.py:29
  47.7 99.7 %collective-permute-start.6 = (bf16[128,1152]{1,0:T(8,128)(2,1)}, bf16[128,1152]{1,0:T(8,128)(2,1)}, u32[]{:S(2)}, u32[]{:S(2)}) collective-permute-start(bf16[128,1152]{1,0:T(8,128)(2,1)} %bitcast.12), channel_id=1, source_target_pairs={{0,8},{8,16},{16,24},{24,32},{32,40},{40,48},{48,56},{56,64},{64,7... | collective-permute-start | bytes 884744 | tf_op jit(solution)/shard_map/ppermute | solution.py:29
  59.0 4.1 copy-start.7
  59.0 4.0 copy-start.26
  73.5 10.9 %copy-start.10 = (bf16[1280,288]{0,1:T(8,128)(2,1)}, bf16[1280,288]{0,1:T(8,128)(2,1)S(1)}, u32[]{:S(2)}) copy-start(bf16[1280,288]{0,1:T(8,128)(2,1)S(1)} %copy.63) | copy-start | bytes 2211844
  88.0 3.1 copy-start.15
  93.1 2.9 copy-start.12
  99.5 3.0 copy-start.16
  119.9 12.7 %copy-start.44 = (s32[7]{0:T(128)S(1)}, s32[7]{0:T(128)}, u32[]{:S(2)}) copy-start(s32[7]{0:T(128)} %copy-done.43) | copy-start | bytes 88
  122.3 129.9 %collective-permute-start.11 = (f32[128,1152]{1,0:T(8,128)}, f32[128,1152]{1,0:T(8,128)}, u32[]{:S(2)}, u32[]{:S(2)}) collective-permute-start(f32[128,1152]{1,0:T(8,128)} %get-tuple-element.29), channel_id=1, source_target_pairs={{0,8},{8,16},{16,24},{24,32},{32,40},{40,48},{48,56},{56,64},{64,7... | collective-permute-start | bytes 1769480 | tf_op jit(solution)/shard_map/ppermute | solution.py:29
  124.2 128.0 %collective-permute-start.10 = (f32[128,1152]{1,0:T(8,128)}, f32[128,1152]{1,0:T(8,128)}, u32[]{:S(2)}, u32[]{:S(2)}) collective-permute-start(f32[128,1152]{1,0:T(8,128)} %get-tuple-element.28), channel_id=1, source_target_pairs={{8,0},{16,8},{24,16},{32,24},{40,32},{48,40},{56,48},{64,56},{72,6... | collective-permute-start | bytes 1769480 | tf_op jit(solution)/shard_map/ppermute | solution.py:29
  138.5 105.0 %all-to-all-start.1 = ((bf16[8,128,1152]{2,1,0:T(8,128)(2,1)}), bf16[8,128,1152]{2,1,0:T(8,128)(2,1)}, u32[]{:S(2)}, u32[]{:S(2)}) async-start(bf16[8,128,1152]{2,1,0:T(8,128)(2,1)} %scatter_fusion.1), calls=%async_computation.1 | async-start | bytes 4718592 | tf_op jit(solution)/shard_map/all_to_all | solution.py:174
  156.2 3.6 copy-start.13
  164.1 3.7 copy-start.11
  172.0 3.6 copy-start.9
  178.6 3.0 copy-start.19
  199.6 2.8 copy-start.23
  205.8 2.8 copy-start.22
  225.6 12.7 %copy-start.45 = (s32[7]{0:T(128)S(1)}, s32[7]{0:T(128)}, u32[]{:S(2)}) copy-start(s32[7]{0:T(128)} %copy-done.43) | copy-start | bytes 88
  228.0 205.7 %collective-permute-start.9 = (f32[128,1152]{1,0:T(8,128)}, f32[128,1152]{1,0:T(8,128)}, u32[]{:S(2)}, u32[]{:S(2)}) collective-permute-start(f32[128,1152]{1,0:T(8,128)} %get-tuple-element.31), channel_id=1, source_target_pairs={{0,8},{8,16},{16,24},{24,32},{32,40},{40,48},{48,56},{56,64},{64,7... | collective-permute-start | bytes 1769480 | tf_op jit(solution)/shard_map/ppermute | solution.py:29
  229.9 203.8 %collective-permute-start.8 = (f32[128,1152]{1,0:T(8,128)}, f32[128,1152]{1,0:T(8,128)}, u32[]{:S(2)}, u32[]{:S(2)}) collective-permute-start(f32[128,1152]{1,0:T(8,128)} %get-tuple-element.30), channel_id=1, source_target_pairs={{8,0},{16,8},{24,16},{32,24},{40,32},{48,40},{56,48},{64,56},{72,6... | collective-permute-start | bytes 1769480 | tf_op jit(solution)/shard_map/ppermute | solution.py:29
  243.5 5.5 %copy-start.42 = (pred[8]{0:T(512)(128)(4,1)S(1)}, pred[8]{0:T(512)(128)(4,1)}, u32[]{:S(2)}) copy-start(pred[8]{0:T(512)(128)(4,1)} %fusion.80) | copy-start | bytes 28
  243.5 186.8 %all-to-all-start = ((bf16[8,128,1152]{2,1,0:T(8,128)(2,1)}), bf16[8,128,1152]{2,1,0:T(8,128)(2,1)}, u32[]{:S(2)}, u32[]{:S(2)}) async-start(bf16[8,128,1152]{2,1,0:T(8,128)(2,1)} %scatter_fusion), calls=%async_computation | async-start | bytes 4718592 | tf_op jit(solution)/shard_map/all_to_all | solution.py:173
  253.7 182.2 %copy-start.3 = (bf16[128,1152]{1,0:T(8,128)(2,1)}, bf16[128,1152]{1,0:T(8,128)(2,1)S(1)}, u32[]{:S(2)}) copy-start(bf16[128,1152]{1,0:T(8,128)(2,1)S(1)} %fusion.76) | copy-start | bytes 884740
  253.8 169.5 %collective-permute-start.13 = (bf16[1,64,1152]{2,1,0:T(8,128)(2,1)S(1)}, bf16[1,64,1152]{2,1,0:T(8,128)(2,1)S(1)}, u32[]{:S(2)}, u32[]{:S(2)}) collective-permute-start(bf16[1,64,1152]{2,1,0:T(8,128)(2,1)S(1)} %get-tuple-element.45), channel_id=1, source_target_pairs={{8,0},{16,8},{24,16},{32,24},{40,32},{48,40},{56,48},{64,56},{72,6... | collective-permute-start | bytes 442376 | tf_op jit(solution)/shard_map/ppermute | solution.py:21
  255.7 167.6 %collective-permute-start.12 = (bf16[1,64,1152]{2,1,0:T(8,128)(2,1)S(1)}, bf16[1,64,1152]{2,1,0:T(8,128)(2,1)S(1)}, u32[]{:S(2)}, u32[]{:S(2)}) collective-permute-start(bf16[1,64,1152]{2,1,0:T(8,128)(2,1)S(1)} %get-tuple-element.44), channel_id=1, source_target_pairs={{0,8},{8,16},{16,24},{24,32},{32,40},{40,48},{48,56},{56,64},{64,7... | collective-permute-start | bytes 442376 | tf_op jit(solution)/shard_map/ppermute | solution.py:18
  423.3 12.6 %collective-permute-start.15 = (bf16[4,1,1152]{2,1,0:T(2,128)(2,1)S(1)}, bf16[4,1,1152]{2,1,0:T(2,128)(2,1)S(1)}, u32[]{:S(2)}, u32[]{:S(2)}) collective-permute-start(bf16[4,1,1152]{2,1,0:T(2,128)(2,1)S(1)} %get-tuple-element.41), channel_id=1, source_target_pairs={{1,0},{2,1},{3,2},{4,3},{5,4},{6,5},{7,6},{9,8},{10,9},{11,10},{12... | collective-permute-start | bytes 27656 | tf_op jit(solution)/shard_map/ppermute | solution.py:21
  428.4 7.6 %collective-permute-start.14 = (bf16[4,1,1152]{2,1,0:T(2,128)(2,1)S(1)}, bf16[4,1,1152]{2,1,0:T(2,128)(2,1)S(1)}, u32[]{:S(2)}, u32[]{:S(2)}) collective-permute-start(bf16[4,1,1152]{2,1,0:T(2,128)(2,1)S(1)} %get-tuple-element.40), channel_id=1, source_target_pairs={{0,1},{1,2},{2,3},{3,4},{4,5},{5,6},{6,7},{8,9},{9,10},{10,11},{11... | collective-permute-start | bytes 27656 | tf_op jit(solution)/shard_map/ppermute | solution.py:18
  (20 other events, 36.6 us)
Sparse Core Ops, SparseCore 0:
  9.8 30.0 all-gather.2
  49.8 29.1 all-gather.4
